TPU v7x, 32 devices: a whole 2x2x4 slice. The times are simulated.
32 devices in a mesh: proto: 8 (over z, x), design: 4 (over y, core).
Axes of the slice: x: 2, y: 2, z: 4, core: 2. Of those that a mesh axis runs over, the one named last changes fastest.
Arguments:
- designs: bfloat16 [32768, 1024], P(('proto', 'design')), may hold values from -32 to 32
- prototypes: float32 [16384, 1024], P('proto'), may hold values from -6 to 6
- candidates: int32 [32, 24], P(('proto', 'design')), may hold values from 0 to 127, as said below
- positives: int32 [32768], P(('proto', 'design')), may hold values from 0 to 16383, as said below
Outputs:
- losses: float32 [32768], P(('proto', 'design'))
- design_grad: bfloat16 [32768, 1024], P(('proto', 'design'))
- proto_grad: float32 [16384, 1024], P(('proto', 'design'))
Inputs may be any that keep to these rules, and one draw needn't show every extreme that they name: `candidates`: row g lists 24 distinct blocks for the designs of device g along proto+design. Block b lies in proto shard b // 16; at most 4 blocks of a row lie in one proto shard, and in every draw one shard holds exactly 4 blocks of every row. `positives`: the positive row of design i lies in one of the blocks of row i // 1024 of candidates.
All inputs are finite; a program needn't handle non-finite values.
Results may differ from a plain program's by a relative error of at most 0.0062.
Values may be sent and summed in bfloat16 or wider, within the bound.
No kernel may reach another device: no remote copies, remote signals or barrier semaphores. Data moves between devices by JAX's collectives and lax.ppermute only.
A program may use at most 128 MiB of HBM per device.

v0:
```python
import jax
import jax.numpy as jnp
from jax import lax
from jax.sharding import PartitionSpec as P

D = 1024
TILE = 128


def contrast(design_rows, cand_rows, block_list, positive_ids):
    logit_scale = D ** (-0.5)
    logits = (
        lax.dot_general(
            design_rows, cand_rows, (((1,), (1,)), ((), ())), preferred_element_type=jnp.float32
        )
        * logit_scale
    )
    cand_count = block_list.shape[0]
    block_match = (positive_ids // TILE)[:, None] == block_list[None, :]
    cand_index = jnp.sum(
        jnp.where(block_match, jnp.arange(cand_count, dtype=jnp.int32)[None, :], 0), axis=1
    )
    positive_col = cand_index * TILE + positive_ids % TILE
    columns = jnp.arange(cand_count * TILE, dtype=jnp.int32)
    target = columns[None, :] == positive_col[:, None]
    row_max = jnp.max(logits, axis=1, keepdims=True)
    log_total = row_max + jnp.log(jnp.sum(jnp.exp(logits - row_max), axis=1, keepdims=True))
    picked = jnp.sum(jnp.where(target, logits, 0.0), axis=1)
    losses = log_total[:, 0] - picked
    chances = jnp.exp(logits - log_total)
    logit_grad = (chances - target.astype(jnp.float32)).astype(jnp.bfloat16)
    design_grad = jnp.dot(logit_grad, cand_rows, preferred_element_type=jnp.float32).astype(
        jnp.bfloat16
    )
    return (losses, design_grad, logit_grad)


def slot_plan(block_list, blocks_dev, capacity, proto_count):
    owners = block_list // blocks_dev
    local_ids = block_list % blocks_dev
    cand_count = block_list.shape[0]
    cand_ids = jnp.arange(cand_count, dtype=jnp.int32)
    same_owner = owners[:, None] == owners[None, :]
    earlier = cand_ids[None, :] < cand_ids[:, None]
    rank_of = jnp.sum(jnp.where(same_owner & earlier, 1, 0), axis=1).astype(jnp.int32)
    slot_of = owners * capacity + rank_of
    hit_table = slot_of[None, :] == jnp.arange(proto_count * capacity, dtype=jnp.int32)[:, None]
    requested = jnp.sum(jnp.where(hit_table, local_ids[None, :] + 1, 0), axis=1) - 1
    source = jnp.sum(jnp.where(hit_table, cand_ids[None, :], 0), axis=1)
    filled = jnp.any(hit_table, axis=1)
    return (slot_of, requested, source, filled)


def body(designs, prototypes, candidates, positives):
    proto_count = lax.axis_size("proto")
    cand_count = candidates.shape[1]
    blocks_dev = prototypes.shape[0] // TILE
    feature_width = designs.shape[1]
    design_count = designs.shape[0]
    capacity = max(2, (4 * cand_count + 3 * proto_count - 1) // (3 * proto_count))
    slot_total = proto_count * capacity
    own_list = candidates[0]
    slot_of, requested, source, filled = slot_plan(own_list, blocks_dev, capacity, proto_count)
    everyone = lax.all_gather(designs, "proto", axis=0, tiled=True)
    incoming = lax.all_to_all(requested, "proto", split_axis=0, concat_axis=0, tiled=True)
    proto_table = prototypes.astype(jnp.bfloat16).reshape(blocks_dev, TILE, feature_width)
    fetched = jnp.take(proto_table, jnp.maximum(incoming, 0), axis=0)
    outgoing = jnp.where((incoming >= 0)[:, None, None], fetched, jnp.zeros((), jnp.bfloat16))
    arrived = lax.all_to_all(outgoing, "proto", split_axis=0, concat_axis=0, tiled=True)
    cand_rows = jnp.take(arrived, slot_of, axis=0).reshape(cand_count * TILE, feature_width)
    losses, design_grad, logit_grad = contrast(designs, cand_rows, own_list, positives)
    slab_rows = logit_grad.T.reshape(cand_count, TILE, design_count)
    outgoing_slab = jnp.where(
        filled[:, None, None], jnp.take(slab_rows, source, axis=0), jnp.zeros((), jnp.bfloat16)
    )
    received = lax.all_to_all(outgoing_slab, "proto", split_axis=0, concat_axis=0, tiled=True)
    returned = jnp.einsum(
        "pctb,pbd->pctd",
        received.reshape(proto_count, capacity, TILE, design_count),
        everyone.reshape(proto_count, design_count, feature_width),
        preferred_element_type=jnp.float32,
    )
    selector = (incoming[None, :] == jnp.arange(blocks_dev, dtype=jnp.int32)[:, None]).astype(
        jnp.float32
    )
    summed = jnp.dot(
        selector,
        returned.reshape(slot_total, TILE * feature_width),
        precision=lax.Precision.HIGHEST,
        preferred_element_type=jnp.float32,
    )
    summed = summed.reshape(blocks_dev * TILE, feature_width)
    owned_rows = lax.psum_scatter(summed, "design", scatter_dimension=0, tiled=True)
    return (losses, design_grad, owned_rows)


def solution(mesh):
    return jax.shard_map(
        body,
        mesh=mesh,
        in_specs=(
            P(("proto", "design"), None),
            P("proto", None),
            P(("proto", "design"), None),
            P(("proto", "design")),
        ),
        out_specs=(
            P(("proto", "design")),
            P(("proto", "design"), None),
            P(("proto", "design"), None),
        ),
        check_vma=False,
    )
```

profile of v0, /device:TPU:0, one launch (start us, length us, event | category | flops | bytes accessed | tf_op | source)
XLA Modules:
  0.0 743.1 jit_solution(12302184155922317201)
XLA Ops:
  7.2 0.7 and_select_fusion.3
  7.8 0.7 fusion.22
  8.5 0.2 select_reduce_fusion.3
  8.7 0.1 select_reduce_fusion.1
  8.8 0.7 sub.53
  9.5 7.3 all-to-all-start
  16.7 6.0 convert_element_type.19
  22.7 0.4 all-to-all-done
  23.2 0.5 broadcast.314
  23.7 0.7 fusion.27
  24.5 7.2 gather_fusion
  31.7 7.6 %select_select_fusion.1 = bf16[32,128,1024]{2,1,0:T(8,128)(2,1)} fusion(bf16[32,128,1024]{2,1,0:T(8,128)(2,1)} %gather_fusion, pred[32]{0:T(512)(128)(4,1)S(1)} %get-tuple-element.12, pred[32]{0:T(512)(128)(4,1)S(1)} %get-tuple-element.11), kind=kLoop, calls=%fused_computation.17 | loop fusion | flops 8388608 | bytes 16777280 | tf_op jit(solution)/shard_map/jit(_where)/select_n | solution.py:68
  39.3 5.7 all-to-all-start.1
  45.0 0.7 all-gather.2.cloned.1.call-update
  45.8 0.1 fusion.14
  46.1 341.6 %all-to-all-done.1 = bf16[32,128,1024]{2,1,0:T(8,128)(2,1)} async-done(((bf16[32,128,1024]{2,1,0:T(8,128)(2,1)}), bf16[32,128,1024]{2,1,0:T(8,128)(2,1)}, u32[]{:S(2)}, u32[]{:S(2)}) %all-to-all-start.1) | async-done | bytes 8388640 | tf_op jit(solution)/shard_map/all_to_all | solution.py:69
  387.7 8.1 %gather_fusion.1 = bf16[24,128,1024]{2,1,0:T(8,128)(2,1)} fusion(bf16[32,128,1024]{2,1,0:T(8,128)(2,1)} %all-to-all-done.1, s32[1024]{0:T(1024)S(1)} %pad_clamp_fusion.1), kind=kCustom, calls=%fused_computation.1 | custom fusion | bytes 12583008 | tf_op jit(solution)/shard_map/jit(_take)/gather | solution.py:70
  395.8 4.0 bitcast_select_fusion.1
  399.8 6.8 multiply_reduce_fusion
  406.6 3.6 fusion.2
  410.3 1.1 fusion.28
  411.4 5.1 subtract_convert_fusion
  416.5 7.8 %gather_fusion.2 = bf16[32,128,1024]{2,1,0:T(8,128)(2,1)} fusion(bf16[24,128,1024]{2,1,0:T(8,128)(2,1)} %bitcast.77, s32[1024]{0:T(1024)S(1)} %pad_clamp_fusion), kind=kCustom, calls=%fused_computation.2 | custom fusion | bytes 16777344 | tf_op jit(solution)/shard_map/jit(_take)/gather | solution.py:74
  424.3 7.6 %select_select_fusion = bf16[32,128,1024]{2,1,0:T(8,128)(2,1)} fusion(bf16[32,128,1024]{2,1,0:T(8,128)(2,1)} %gather_fusion.2, pred[32]{0:T(512)(128)(4,1)S(1)} %compare_and_fusion, pred[32]{0:T(512)(128)(4,1)S(1)} %fusion.14), kind=kLoop, calls=%fused_computation.16 | loop fusion | flops 8388608 | bytes 16777280 | tf_op jit(solution)/shard_map/jit(_where)/select_n | solution.py:73
  431.9 5.2 all-to-all-start.2
  437.1 179.5 %all-to-all-done.2 = bf16[32,128,1024]{2,1,0:T(8,128)(2,1)} async-done(((bf16[32,128,1024]{2,1,0:T(8,128)(2,1)}), bf16[32,128,1024]{2,1,0:T(8,128)(2,1)}, u32[]{:S(2)}, u32[]{:S(2)}) %all-to-all-start.2) | async-done | bytes 8388640 | tf_op jit(solution)/shard_map/all_to_all | solution.py:76
  616.6 19.3 %fusion.29 = f32[8,4,128,1024]{3,2,1,0:T(8,128)} fusion(bf16[8,4,128,1024]{3,2,1,0:T(8,128)(2,1)} %bitcast.16, bf16[8,1024,1024,1]{2,1,3,0:T(8,128)(2,1)} %bitcast.80), kind=kOutput, calls=%fused_computation.83 | convolution fusion | flops 8589934592 | bytes 41943040 | tf_op jit(solution)/shard_map/pctb,pbd->pctd/dot_general | solution.py:77
  635.9 15.2 %copy.10 = f32[4,8,128,1024]{3,1,2,0:T(8,128)S(1)} copy(f32[4,8,128,1024]{3,2,1,0:T(8,128)} %bitcast.78) | data formatting | bytes 33554432
  651.1 8.1 %fusion.16 = f32[16,131072]{1,0:T(8,128)} fusion(f32[32,131072]{1,0:T(8,128)S(1)} %bitcast.75, s32[32]{0:T(128)S(1)} %all_to_all.13), kind=kOutput, calls=%fused_computation.33 | convolution fusion | flops 805306880 | bytes 25165952 | tf_op jit(solution)/shard_map/dot_general | solution.py:86
  659.3 6.2 reshape.208
  665.5 14.5 %fusion.11 = bf16[1024,1024]{1,0:T(8,128)(2,1)} fusion(bf16[3072,1024]{1,0:T(8,128)(2,1)} %copy-done.1, f32[3072,1024]{1,0:T(8,128)} %copy-done, f32[1024]{0:T(1024)S(1)} %get-tuple-element.10, s32[1024]{0:T(1024)S(1)} %fusion.17), kind=kOutput, calls=%fused_computation.23 | convolution fusion | flops 6462373888 | bytes 20979712 | tf_op jit(solution)/shard_map/dot_general | solution.py:32
  679.9 56.3 %reduce-scatter.2.cloned.1.call-done = f32[512,1024]{1,0:T(8,128)} async-done(((f32[2048,1024]{1,0:T(8,128)}), f32[512,1024]{1,0:T(8,128)}) %reduce-scatter.2.cloned.1.call-update) | async-done | bytes 2097168 | tf_op jit(solution)/shard_map/reduce_scatter | solution.py:93
  (30 shorter events, 0.6 us)
Async XLA Ops:
  9.5 13.7 %all-to-all-start = ((s32[8,4,1]{1,2,0:T(1,128)}), s32[8,4,1]{1,2,0:T(1,128)S(1)}, u32[]{:S(2)}, u32[]{:S(2)}) async-start(s32[8,4,1]{1,2,0:T(1,128)} %bitcast.6), calls=%async_computation | async-start | bytes 8192 | tf_op jit(solution)/shard_map/all_to_all | solution.py:65
  39.3 6.4 copy-start.4
  39.3 6.6 copy-start.3
  39.3 348.4 %all-to-all-start.1 = ((bf16[32,128,1024]{2,1,0:T(8,128)(2,1)}), bf16[32,128,1024]{2,1,0:T(8,128)(2,1)}, u32[]{:S(2)}, u32[]{:S(2)}) async-start(bf16[32,128,1024]{2,1,0:T(8,128)(2,1)} %select_select_fusion.1), calls=%async_computation.1 | async-start | bytes 16777216 | tf_op jit(solution)/shard_map/all_to_all | solution.py:69
  45.0 392.1 %all-gather.2.cloned.1.call-start = ((), (), s32[]{:S(2)}) async-start(), calls=%async_computation.4 | async-start | bytes 18874368 | tf_op jit(solution)/shard_map/all_gather | solution.py:64
  395.8 4.0 copy-start.2
  399.8 6.8 copy-start.1
  406.6 9.9 %copy-start = (f32[3072,1024]{1,0:T(8,128)}, f32[3072,1024]{1,0:T(8,128)S(1)}, u32[]{:S(2)}) copy-start(f32[3072,1024]{1,0:T(8,128)S(1)} %get-tuple-element.16) | copy-start | bytes 37748740
  431.9 184.7 %all-to-all-start.2 = ((bf16[32,128,1024]{2,1,0:T(8,128)(2,1)}), bf16[32,128,1024]{2,1,0:T(8,128)(2,1)}, u32[]{:S(2)}, u32[]{:S(2)}) async-start(bf16[32,128,1024]{2,1,0:T(8,128)(2,1)} %select_select_fusion), calls=%async_computation.2 | async-start | bytes 16777216 | tf_op jit(solution)/shard_map/all_to_all | solution.py:76
  437.1 299.2 %reduce-scatter.2.cloned.1.call-start = ((), (), s32[]{:S(2)}) async-start(), calls=%async_computation.5 | async-start | bytes 10485760 | tf_op jit(solution)/shard_map/reduce_scatter | solution.py:93
Sparse Core Ops, SparseCore 0:
  47.9 388.1 all-gather.1
  665.6 70.6 reduce-scatter.1
where the time goes:
time: 744 us; the launch traced here: 743 us
  waiting for transfers between devices  579 us (78%)
  matrix products  48.7 us (7%)
  local copies, waits for them, and re-layouts  45.9 us (6%)
  other arithmetic  37.5 us (5%)
  starting transfers between devices  18.2 us (2%)
  between operations  14.2 us (2%)
    all_to_all x1, waiting for transfers between devices, body(): lax.all_to_all(outgoing, 'proto', split_axis=0, concat_axis=0, tiled=True)  342 us
    all_to_all x1, waiting for transfers between devices, body(): lax.all_to_all(outgoing_slab, 'proto', split_axis=0, concat_axis=0, tiled...  179 us
    reduce_scatter x1, waiting for transfers between devices, body(): lax.psum_scatter(summed, 'design', scatter_dimension=0, tiled=True)  56.3 us
    dot_general x1, matrix products, body(): jnp.einsum('pctb,pbd->pctd', received.reshape(proto_count, capacity, TILE...  19.3 us
    unnamed x11, local copies, waits for them, and re-layouts  15.2 us
  transfers between devices with their start and end apart: 5, of which 4 were waited for; matrix products, arithmetic and copies ran while one was open for 9% of the time, Pallas kernels for 0%

commit v1 on v0

--- a/solution.py
+++ b/solution.py
@@ -5,6 +5,22 @@
 
 D = 1024
 TILE = 128
+
+
+def pairwise_exchange(shard, axis, split, join):
+    ways, here = (lax.axis_size(axis), lax.axis_index(axis))
+    width = shard.shape[split] // ways
+    shape = list(shard.shape)
+    shape[split] = width
+    height = shape[join]
+    shape[join] = height * ways
+    full = jnp.zeros(shape, shard.dtype)
+    for mask in range(ways):
+        part = lax.dynamic_slice_in_dim(shard, (here ^ mask) * width, width, axis=split)
+        if mask:
+            part = lax.ppermute(part, axis, [(d, d ^ mask) for d in range(ways)])
+        full = lax.dynamic_update_slice_in_dim(full, part, (here ^ mask) * height, axis=join)
+    return full
 
 
 def contrast(design_rows, cand_rows, block_list, positive_ids):
@@ -66,7 +82,7 @@
     proto_table = prototypes.astype(jnp.bfloat16).reshape(blocks_dev, TILE, feature_width)
     fetched = jnp.take(proto_table, jnp.maximum(incoming, 0), axis=0)
     outgoing = jnp.where((incoming >= 0)[:, None, None], fetched, jnp.zeros((), jnp.bfloat16))
-    arrived = lax.all_to_all(outgoing, "proto", split_axis=0, concat_axis=0, tiled=True)
+    arrived = pairwise_exchange(outgoing, "proto", 0, 0)
     cand_rows = jnp.take(arrived, slot_of, axis=0).reshape(cand_count * TILE, feature_width)
     losses, design_grad, logit_grad = contrast(designs, cand_rows, own_list, positives)
     slab_rows = logit_grad.T.reshape(cand_count, TILE, design_count)

time: 744 us -> 744 us (level)
  waiting for transfers between devices: 579 us -> 281 us
  blocking collectives: 0 us -> 277 us
  local copies, waits for them, and re-layouts: 45.9 us -> 62.1 us
    all_to_all x2 -> x0, waiting for transfers between devices: 521 us -> none  [the longest x1 342 us: body(): lax.all_to_all(outgoing, 'proto', split_axis=0, concat_axis=0, tiled=True)]
    all_to_all x0 -> x1, blocking collectives: none -> 277 us  [body(): lax.all_to_all(outgoing_slab, 'proto', split_axis=0, concat_axis=0, tiled...]
    ppermute x0 -> x7, waiting for transfers between devices: none -> 224 us  [pairwise_exchange(): part = lax.ppermute(part, axis, [(d, d ^ mask) for d in range(ways)])]
    ppermute x0 -> x7, starting transfers between devices: none -> 14.4 us  [pairwise_exchange(): part = lax.ppermute(part, axis, [(d, d ^ mask) for d in range(ways)])]
    all_to_all x2 -> x0, starting transfers between devices: 10.9 us -> none  [the longest x1 5.71 us: body(): lax.all_to_all(outgoing, 'proto', split_axis=0, concat_axis=0, tiled=True)]
    dynamic_update_slice x0 -> x7, local copies, waits for them, and re-layouts: none -> 7.45 us  [pairwise_exchange(): lax.dynamic_update_slice_in_dim(full, part, (here ^ mask) * height, axis=...]
    unnamed x11 -> x13, local copies, waits for them, and re-layouts: 15.2 us -> 16.3 us
  transfers between devices with their start and end apart: 5 -> 10, of which waited for: 4 -> 6; matrix products, arithmetic and copies ran while one was open for 9% -> 13% of each run, Pallas kernels for 0% -> 0%
where the time goes in v1:
time: 744 us
  waiting for transfers between devices  281 us (38%)
  blocking collectives  277 us (37%)
  local copies, waits for them, and re-layouts  62.1 us (8%)
  matrix products  48.7 us (7%)
  other arithmetic  38.4 us (5%)
  starting transfers between devices  21.7 us (3%)
  between operations  14.2 us (2%)
    all_to_all x1, blocking collectives, body(): lax.all_to_all(outgoing_slab, 'proto', split_axis=0, concat_axis=0, tiled...  277 us
    ppermute x7, waiting for transfers between devices, pairwise_exchange(): part = lax.ppermute(part, axis, [(d, d ^ mask) for d in range(ways)])  224 us
    reduce_scatter x1, waiting for transfers between devices, body(): lax.psum_scatter(summed, 'design', scatter_dimension=0, tiled=True)  56.6 us
    dot_general x1, matrix products, body(): jnp.einsum('pctb,pbd->pctd', received.reshape(proto_count, capacity, TILE...  19.3 us
    unnamed x13, local copies, waits for them, and re-layouts  16.3 us
  transfers between devices with their start and end apart: 10, of which 6 were waited for; matrix products, arithmetic and copies ran while one was open for 13% of the time, Pallas kernels for 0%

profile of v1, /device:TPU:0, one launch (start us, length us, event | category | flops | bytes accessed | tf_op | source)
XLA Modules:
  0.0 743.8 jit_solution(7865465587034532176)
XLA Ops:
  10.2 7.3 all-to-all-start
  17.6 6.7 convert_element_type.19
  25.6 7.2 gather_fusion
  32.8 7.6 %select_select_fusion.1 = bf16[32,128,1024]{2,1,0:T(8,128)(2,1)} fusion(bf16[32,128,1024]{2,1,0:T(8,128)(2,1)} %gather_fusion, pred[32]{0:T(512)(128)(4,1)S(1)} %get-tuple-element.20, pred[32]{0:T(512)(128)(4,1)S(1)} %get-tuple-element.19), kind=kLoop, calls=%fused_computation.17 | loop fusion | flops 8388608 | bytes 16777280 | tf_op jit(solution)/shard_map/jit(_where)/select_n | solution.py:84
  40.5 5.3 broadcast_in_dim.118
  45.8 1.1 copy-done.1
  46.9 2.5 constant_dynamic-slice_fusion
  49.4 2.1 collective-permute-start
  51.5 1.4 collective-permute-start.1
  53.2 2.8 collective-permute-start.3
  56.0 1.6 collective-permute-start.4
  57.6 16.3 %collective-permute-done = bf16[4,128,1024]{2,1,0:T(8,128)(2,1)S(1)} collective-permute-done((bf16[4,128,1024]{2,1,0:T(8,128)(2,1)S(1)}, bf16[4,128,1024]{2,1,0:T(8,128)(2,1)S(1)}, u32[]{:S(2)}, u32[]{:S(2)}) %collective-permute-start) | collective-permute-done | bytes 1048608 | tf_op jit(solution)/shard_map/ppermute | solution.py:21
  73.9 3.2 collective-permute-start.5
  77.2 83.3 %collective-permute-done.1 = bf16[4,128,1024]{2,1,0:T(8,128)(2,1)S(1)} collective-permute-done((bf16[4,128,1024]{2,1,0:T(8,128)(2,1)S(1)}, bf16[4,128,1024]{2,1,0:T(8,128)(2,1)S(1)}, u32[]{:S(2)}, u32[]{:S(2)}) %collective-permute-start.1) | collective-permute-done | bytes 1048608 | tf_op jit(solution)/shard_map/ppermute | solution.py:21
  160.5 3.1 collective-permute-start.6
  165.9 43.0 %collective-permute-done.2 = bf16[4,128,1024]{2,1,0:T(8,128)(2,1)S(1)} collective-permute-done((bf16[4,128,1024]{2,1,0:T(8,128)(2,1)S(1)}, bf16[4,128,1024]{2,1,0:T(8,128)(2,1)S(1)}, u32[]{:S(2)}, u32[]{:S(2)}) %collective-permute-start.2) | collective-permute-done | bytes 1048608 | tf_op jit(solution)/shard_map/ppermute | solution.py:21
  212.0 37.3 %collective-permute-done.5 = bf16[4,128,1024]{2,1,0:T(8,128)(2,1)S(1)} collective-permute-done((bf16[4,128,1024]{2,1,0:T(8,128)(2,1)S(1)}, bf16[4,128,1024]{2,1,0:T(8,128)(2,1)S(1)}, u32[]{:S(2)}, u32[]{:S(2)}) %collective-permute-start.5) | collective-permute-done | bytes 1048608 | tf_op jit(solution)/shard_map/ppermute | solution.py:21
  250.4 44.1 %collective-permute-done.6 = bf16[4,128,1024]{2,1,0:T(8,128)(2,1)S(1)} collective-permute-done((bf16[4,128,1024]{2,1,0:T(8,128)(2,1)S(1)}, bf16[4,128,1024]{2,1,0:T(8,128)(2,1)S(1)}, u32[]{:S(2)}, u32[]{:S(2)}) %collective-permute-start.6) | collective-permute-done | bytes 1048608 | tf_op jit(solution)/shard_map/ppermute | solution.py:21
  295.6 7.9 %gather_fusion.1 = bf16[24,128,1024]{2,1,0:T(8,128)(2,1)} fusion(bf16[32,128,1024]{2,1,0:T(8,128)(2,1)} %constant_dynamic-update-slice_fusion, s32[1024]{0:T(1024)S(1)} %pad_clamp_fusion.1), kind=kCustom, calls=%fused_computation.1 | custom fusion | bytes 12583008 | tf_op jit(solution)/shard_map/jit(_take)/gather | solution.py:86
  303.5 4.2 bitcast_select_fusion.1
  307.7 6.8 multiply_reduce_fusion
  314.5 3.6 fusion.2
  319.2 5.1 subtract_convert_fusion
  324.4 7.8 %gather_fusion.2 = bf16[32,128,1024]{2,1,0:T(8,128)(2,1)} fusion(bf16[24,128,1024]{2,1,0:T(8,128)(2,1)} %bitcast.77, s32[1024]{0:T(1024)S(1)} %pad_clamp_fusion), kind=kCustom, calls=%fused_computation.2 | custom fusion | bytes 16777344 | tf_op jit(solution)/shard_map/jit(_take)/gather | solution.py:90
  332.2 7.6 %select_select_fusion = bf16[32,128,1024]{2,1,0:T(8,128)(2,1)} fusion(bf16[32,128,1024]{2,1,0:T(8,128)(2,1)} %gather_fusion.2, pred[32]{0:T(512)(128)(4,1)S(1)} %get-tuple-element.25, pred[32]{0:T(512)(128)(4,1)S(1)} %fusion.14), kind=kLoop, calls=%fused_computation.16 | loop fusion | flops 8388608 | bytes 16777280 | tf_op jit(solution)/shard_map/jit(_where)/select_n | solution.py:89
  339.8 277.3 %all_to_all.14 = bf16[32,128,1024]{2,1,0:T(8,128)(2,1)} all-to-all(bf16[32,128,1024]{2,1,0:T(8,128)(2,1)} %select_select_fusion), channel_id=1, replica_groups=mesh['proto'=8,'design'=4] {'proto'}, dimensions={0} | all-to-all | bytes 16777216 | tf_op jit(solution)/shard_map/all_to_all | solution.py:92
  617.1 19.3 %fusion.29 = f32[8,4,128,1024]{3,2,1,0:T(8,128)} fusion(bf16[8,4,128,1024]{3,2,1,0:T(8,128)(2,1)} %bitcast.79, bf16[8,1024,1024,1]{2,1,3,0:T(8,128)(2,1)} %bitcast.81), kind=kOutput, calls=%fused_computation.98 | convolution fusion | flops 8589934592 | bytes 41943040 | tf_op jit(solution)/shard_map/pctb,pbd->pctd/dot_general | solution.py:93
  636.4 15.2 %copy.10 = f32[4,8,128,1024]{3,1,2,0:T(8,128)S(1)} copy(f32[4,8,128,1024]{3,2,1,0:T(8,128)} %bitcast.78) | data formatting | bytes 33554432
  651.6 8.1 %fusion.16 = f32[16,131072]{1,0:T(8,128)} fusion(f32[32,131072]{1,0:T(8,128)S(1)} %bitcast.75, s32[32]{0:T(128)S(1)} %all_to_all.10), kind=kOutput, calls=%fused_computation.34 | convolution fusion | flops 805306880 | bytes 25165952 | tf_op jit(solution)/shard_map/dot_general | solution.py:102
  659.7 6.2 reshape.208
  665.9 14.4 %fusion.11 = bf16[1024,1024]{1,0:T(8,128)(2,1)} fusion(bf16[3072,1024]{1,0:T(8,128)(2,1)} %copy-done.2, f32[3072,1024]{1,0:T(8,128)} %copy-done, f32[1024]{0:T(1024)S(1)} %get-tuple-element.10, s32[1024]{0:T(1024)S(1)} %fusion.17), kind=kOutput, calls=%fused_computation.23 | convolution fusion | flops 6462373888 | bytes 20979712 | tf_op jit(solution)/shard_map/dot_general | solution.py:48
  680.4 56.6 %reduce-scatter.2.cloned.1.call-done = f32[512,1024]{1,0:T(8,128)} async-done(((f32[2048,1024]{1,0:T(8,128)}), f32[512,1024]{1,0:T(8,128)}) %reduce-scatter.2.cloned.1.call-update) | async-done | bytes 2097168 | tf_op jit(solution)/shard_map/reduce_scatter | solution.py:109
  (51 shorter events, 13.5 us)
Async XLA Ops:
  7.2 17.1 %copy-start.4 = (s32[1024]{0:T(1024)S(1)}, s32[1024]{0:T(1024)}, u32[]{:S(2)}) copy-start(s32[1024]{0:T(1024)} %param.7) | copy-start | bytes 12292
  7.2 609.9 %all-gather.2.cloned.1.call-start = ((), (), s32[]{:S(2)}) async-start(), calls=%async_computation.3 | async-start | bytes 18874368 | tf_op jit(solution)/shard_map/all_gather | solution.py:80
  10.2 14.0 %all-to-all-start = ((s32[8,4,1]{1,2,0:T(1,128)}), s32[8,4,1]{1,2,0:T(1,128)S(1)}, u32[]{:S(2)}, u32[]{:S(2)}) async-start(s32[8,4,1]{1,2,0:T(1,128)} %bitcast.6), calls=%async_computation | async-start | bytes 8192 | tf_op jit(solution)/shard_map/all_to_all | solution.py:81
  17.5 719.5 %reduce-scatter.2.cloned.1.call-start = ((), (), s32[]{:S(2)}) async-start(), calls=%async_computation.4 | async-start | bytes 10485760 | tf_op jit(solution)/shard_map/reduce_scatter | solution.py:109
  40.5 6.4 copy-start.1
  46.9 4.6 copy-start.5
  49.4 24.5 %collective-permute-start = (bf16[4,128,1024]{2,1,0:T(8,128)(2,1)S(1)}, bf16[4,128,1024]{2,1,0:T(8,128)(2,1)S(1)}, u32[]{:S(2)}, u32[]{:S(2)}) collective-permute-start(bf16[4,128,1024]{2,1,0:T(8,128)(2,1)S(1)} %get-tuple-element.17), channel_id=1, source_target_pairs={{0,4},{4,0},{8,12},{12,8},{16,20},{20,16},{24,28},{28,24},{1,5},{5... | collective-permute-start | bytes 3145736 | tf_op jit(solution)/shard_map/ppermute | solution.py:21
  51.5 109.0 %collective-permute-start.1 = (bf16[4,128,1024]{2,1,0:T(8,128)(2,1)S(1)}, bf16[4,128,1024]{2,1,0:T(8,128)(2,1)S(1)}, u32[]{:S(2)}, u32[]{:S(2)}) collective-permute-start(bf16[4,128,1024]{2,1,0:T(8,128)(2,1)S(1)} %get-tuple-element.16), channel_id=1, source_target_pairs={{0,8},{4,12},{8,0},{12,4},{16,24},{20,28},{24,16},{28,20},{1,9},{5... | collective-permute-start | bytes 3145736 | tf_op jit(solution)/shard_map/ppermute | solution.py:21
  53.1 155.8 %collective-permute-start.2 = (bf16[4,128,1024]{2,1,0:T(8,128)(2,1)S(1)}, bf16[4,128,1024]{2,1,0:T(8,128)(2,1)S(1)}, u32[]{:S(2)}, u32[]{:S(2)}) collective-permute-start(bf16[4,128,1024]{2,1,0:T(8,128)(2,1)S(1)} %get-tuple-element.15), channel_id=1, source_target_pairs={{0,12},{4,8},{8,4},{12,0},{16,28},{20,24},{24,20},{28,16},{1,13},{... | collective-permute-start | bytes 3145736 | tf_op jit(solution)/shard_map/ppermute | solution.py:21
  53.2 156.7 %collective-permute-start.3 = (bf16[4,128,1024]{2,1,0:T(8,128)(2,1)S(1)}, bf16[4,128,1024]{2,1,0:T(8,128)(2,1)S(1)}, u32[]{:S(2)}, u32[]{:S(2)}) collective-permute-start(bf16[4,128,1024]{2,1,0:T(8,128)(2,1)S(1)} %get-tuple-element.14), channel_id=1, source_target_pairs={{0,16},{4,20},{8,24},{12,28},{16,0},{20,4},{24,8},{28,12},{1,17},{... | collective-permute-start | bytes 3145736 | tf_op jit(solution)/shard_map/ppermute | solution.py:21
  56.0 154.9 %collective-permute-start.4 = (bf16[4,128,1024]{2,1,0:T(8,128)(2,1)S(1)}, bf16[4,128,1024]{2,1,0:T(8,128)(2,1)S(1)}, u32[]{:S(2)}, u32[]{:S(2)}) collective-permute-start(bf16[4,128,1024]{2,1,0:T(8,128)(2,1)S(1)} %get-tuple-element.13), channel_id=1, source_target_pairs={{0,20},{4,16},{8,28},{12,24},{16,4},{20,0},{24,12},{28,8},{1,21},{... | collective-permute-start | bytes 3145736 | tf_op jit(solution)/shard_map/ppermute | solution.py:21
  73.9 175.5 %collective-permute-start.5 = (bf16[4,128,1024]{2,1,0:T(8,128)(2,1)S(1)}, bf16[4,128,1024]{2,1,0:T(8,128)(2,1)S(1)}, u32[]{:S(2)}, u32[]{:S(2)}) collective-permute-start(bf16[4,128,1024]{2,1,0:T(8,128)(2,1)S(1)} %get-tuple-element.12), channel_id=1, source_target_pairs={{0,24},{4,28},{8,16},{12,20},{16,8},{20,12},{24,0},{28,4},{1,25},{... | collective-permute-start | bytes 3145736 | tf_op jit(solution)/shard_map/ppermute | solution.py:21
  160.5 134.1 %collective-permute-start.6 = (bf16[4,128,1024]{2,1,0:T(8,128)(2,1)S(1)}, bf16[4,128,1024]{2,1,0:T(8,128)(2,1)S(1)}, u32[]{:S(2)}, u32[]{:S(2)}) collective-permute-start(bf16[4,128,1024]{2,1,0:T(8,128)(2,1)S(1)} %get-tuple-element.11), channel_id=1, source_target_pairs={{0,28},{4,24},{8,20},{12,16},{16,12},{20,8},{24,4},{28,0},{1,29},{... | collective-permute-start | bytes 3145736 | tf_op jit(solution)/shard_map/ppermute | solution.py:21
  303.5 4.2 copy-start.3
  307.7 6.8 copy-start.2
  314.5 9.9 %copy-start = (f32[3072,1024]{1,0:T(8,128)}, f32[3072,1024]{1,0:T(8,128)S(1)}, u32[]{:S(2)}) copy-start(f32[3072,1024]{1,0:T(8,128)S(1)} %get-tuple-element.24) | copy-start | bytes 37748740
Sparse Core Ops, SparseCore 0:
  10.1 399.7 all-gather.1
  666.0 70.9 reduce-scatter.1
